TPU v7x, 32 devices: a whole 2x2x4 slice. The times are simulated.
32 devices in a mesh: fsdp: 8 (over y, x, core), seq: 4 (over z).
Axes of the slice: x: 2, y: 2, z: 4, core: 2. Of those that a mesh axis runs over, the one named last changes fastest.
Arguments:
- hidden_in: bfloat16 [8, 1024, 2048], P('fsdp', 'seq'), may hold values from -6 to 6
- lengths: int32 [8], P('fsdp'), may hold values from 512 to 1024, as said below
- cotangent: bfloat16 [8, 1024, 2048], P('fsdp', 'seq'), may hold values from -6 to 6
- in_weight: bfloat16 [2048, 6144], P(('fsdp', 'seq')), may hold values from -0.125 to 0.125
- in_bias: bfloat16 [6144], P(('fsdp', 'seq')), may hold values from -0.29882812 to 0.29882812
- out_weight: bfloat16 [2048, 2048], P(('fsdp', 'seq')), may hold values from -1 to 1
- out_bias: bfloat16 [2048], P(('fsdp', 'seq')), may hold values from -2 to 2
- up_weight: bfloat16 [8192, 2048], P(('fsdp', 'seq')), may hold values from -0.125 to 0.125
- up_bias: bfloat16 [8192], P(('fsdp', 'seq')), may hold values from -2 to 2
- down_weight: bfloat16 [8192, 2048], P(('fsdp', 'seq')), may hold values from -0.0625 to 0.0625
- down_bias: bfloat16 [2048], P(('fsdp', 'seq')), may hold values from -2 to 2
- first_gain: bfloat16 [2048], P(('fsdp', 'seq')), may hold values from 0.5 to 1.5
- first_shift: bfloat16 [2048], P(('fsdp', 'seq')), may hold values from -2 to 2
- second_gain: bfloat16 [2048], P(('fsdp', 'seq')), may hold values from 0.5 to 1.5
- second_shift: bfloat16 [2048], P(('fsdp', 'seq')), may hold values from -2 to 2
Outputs:
- layer_output: float32 [8, 1024, 2048], P('fsdp', 'seq')
- input_gradient: float32 [8, 1024, 2048], P('fsdp', 'seq')
- in_weight_gradient: float32 [2048, 6144], P(('fsdp', 'seq'))
- in_bias_gradient: float32 [6144], P(('fsdp', 'seq'))
- out_weight_gradient: float32 [2048, 2048], P(('fsdp', 'seq'))
- out_bias_gradient: float32 [2048], P(('fsdp', 'seq'))
- up_weight_gradient: float32 [8192, 2048], P(('fsdp', 'seq'))
- up_bias_gradient: float32 [8192], P(('fsdp', 'seq'))
- down_weight_gradient: float32 [8192, 2048], P(('fsdp', 'seq'))
- down_bias_gradient: float32 [2048], P(('fsdp', 'seq'))
- first_gain_gradient: float32 [2048], P(('fsdp', 'seq'))
- first_shift_gradient: float32 [2048], P(('fsdp', 'seq'))
- second_gain_gradient: float32 [2048], P(('fsdp', 'seq'))
- second_shift_gradient: float32 [2048], P(('fsdp', 'seq'))
Inputs may be any that keep to these rules, and one draw needn't show every extreme that they name: `lengths`: tokens in use at the front of each slot; in every draw one slot is full and one holds 512 tokens.
All inputs are finite; a program needn't handle non-finite values.
Results may differ from a plain program's by a relative error of at most 0.014.
Values may be sent and summed in bfloat16 or wider, within the bound.
No kernel may reach another device: no remote copies, remote signals or barrier semaphores. Data moves between devices by JAX's collectives and lax.ppermute only.
A program may use at most 384 MiB of HBM per device.

v0:
```python
import jax
import jax.numpy as jnp
from jax import lax
from jax.sharding import PartitionSpec as P

HEADS = 16
HEAD_DIM = 128
ROT = 32
EPSILON = 1e-05
MASKED_SCORE = -1e30


def layer_norm(values, norm_gain, norm_shift):
    centred = values - jnp.mean(values, axis=-1, keepdims=True)
    spread = jnp.mean(centred * centred, axis=-1, keepdims=True)
    return centred * lax.rsqrt(spread + EPSILON) * norm_gain + norm_shift


def rotary_tables(positions):
    halves = jnp.arange(ROT // 2, dtype=jnp.float32)
    frequency = 1.0 / 10000.0 ** (halves * 2.0 / ROT)
    angles = positions.astype(jnp.float32)[:, None] * frequency[None, :]
    angles = jnp.concatenate([angles, angles], axis=1)
    return (jnp.cos(angles), jnp.sin(angles))


def rotate(values, cosine_table, sine_table):
    leading = values[..., :ROT]
    middle = ROT // 2
    turned = jnp.concatenate([-leading[..., middle:], leading[..., :middle]], axis=-1)
    leading = leading * cosine_table[:, None, :] + turned * sine_table[:, None, :]
    return jnp.concatenate([leading, values[..., ROT:]], axis=-1)


def exact_gelu(values):
    return jax.nn.gelu(values, approximate=False)


def matmul(left_side, right_side):
    return jnp.dot(left_side, right_side, preferred_element_type=jnp.float32)


def times_transposed(left_side, right_side):
    return lax.dot_general(
        left_side, right_side, (((1,), (1,)), ((), ())), preferred_element_type=jnp.float32
    )


def transposed_times(left_side, right_side):
    return lax.dot_general(
        left_side, right_side, (((0,), (0,)), ((), ())), preferred_element_type=jnp.float32
    )


def attend_slot(query, key_rows, value_rows, keep_mask):
    length_full = query.shape[0]
    block_rows = min(512, length_full)
    block_count = length_full // block_rows
    columns = jnp.arange(length_full, dtype=jnp.int32)
    scale_factor = HEAD_DIM ** (-0.5)

    def one_block(first_row):
        row_index = first_row + jnp.arange(block_rows, dtype=jnp.int32)
        query_block = lax.dynamic_slice_in_dim(query, first_row, block_rows, 0)
        scores = (
            jnp.einsum("qhd,khd->hqk", query_block, key_rows, preferred_element_type=jnp.float32)
            * scale_factor
        )
        allowed = (columns[None, :] <= row_index[:, None]) & keep_mask[None, :]
        scores = jnp.where(allowed[None], scores, MASKED_SCORE)
        largest = jnp.max(scores, axis=-1, keepdims=True)
        weights = jnp.exp(scores - largest)
        totals = jnp.sum(weights, axis=-1, keepdims=True)
        probabilities = (weights / totals).astype(jnp.bfloat16)
        mixed = jnp.einsum(
            "hqk,khd->qhd", probabilities, value_rows, preferred_element_type=jnp.float32
        )
        return (mixed, (largest + jnp.log(totals))[..., 0])

    starts = jnp.arange(block_count, dtype=jnp.int32) * block_rows
    mixed, log_sums = lax.map(one_block, starts)
    return (mixed.reshape(length_full, query.shape[1], query.shape[2]), log_sums)


def attend_slot_back(query, key_rows, value_rows, keep_mask, log_sums, mixed_delta):
    length_full = query.shape[0]
    block_rows = min(512, length_full)
    block_count = length_full // block_rows
    columns = jnp.arange(length_full, dtype=jnp.int32)
    scale_factor = HEAD_DIM ** (-0.5)

    def one_block(carried, member):
        key_delta, value_delta = carried
        first_row, log_block = member
        row_index = first_row + jnp.arange(block_rows, dtype=jnp.int32)
        query_block = lax.dynamic_slice_in_dim(query, first_row, block_rows, 0)
        delta_block = lax.dynamic_slice_in_dim(mixed_delta, first_row, block_rows, 0)
        scores = (
            jnp.einsum("qhd,khd->hqk", query_block, key_rows, preferred_element_type=jnp.float32)
            * scale_factor
        )
        allowed = (columns[None, :] <= row_index[:, None]) & keep_mask[None, :]
        scores = jnp.where(allowed[None], scores, MASKED_SCORE)
        probabilities = jnp.where(allowed[None], jnp.exp(scores - log_block[..., None]), 0.0)
        prob_delta = jnp.einsum(
            "qhd,khd->hqk", delta_block, value_rows, preferred_element_type=jnp.float32
        )
        row_dot = jnp.sum(probabilities * prob_delta, axis=-1, keepdims=True)
        score_delta = (probabilities * (prob_delta - row_dot)).astype(jnp.bfloat16)
        query_delta = (
            jnp.einsum("hqk,khd->qhd", score_delta, key_rows, preferred_element_type=jnp.float32)
            * scale_factor
        )
        key_delta = (
            key_delta
            + jnp.einsum(
                "hqk,qhd->khd", score_delta, query_block, preferred_element_type=jnp.float32
            )
            * scale_factor
        )
        value_delta = value_delta + jnp.einsum(
            "hqk,qhd->khd",
            probabilities.astype(jnp.bfloat16),
            delta_block,
            preferred_element_type=jnp.float32,
        )
        return ((key_delta, value_delta), query_delta)

    starts = jnp.arange(block_count, dtype=jnp.int32) * block_rows
    zeroes = jnp.zeros(query.shape, jnp.float32)
    (key_delta, value_delta), query_delta = lax.scan(
        one_block, (zeroes, zeroes), (starts, log_sums)
    )
    return (query_delta.reshape(query.shape), key_delta, value_delta)


def feed_forward(inner_in, up_matrix, up_offset, down_matrix):
    hidden_pre = times_transposed(inner_in, up_matrix) + up_offset.astype(jnp.float32)
    hidden_act, pull_act = jax.vjp(exact_gelu, hidden_pre)
    hidden_low = hidden_act.astype(jnp.bfloat16)
    return (hidden_low, pull_act, matmul(hidden_low, down_matrix))


def feed_back(inner_in, hidden_low, pull_act, delta_rows, up_matrix, down_matrix):
    delta_down = transposed_times(hidden_low, delta_rows)
    delta_pre = pull_act(times_transposed(delta_rows, down_matrix))[0].astype(jnp.bfloat16)
    delta_up = transposed_times(delta_pre, inner_in)
    delta_up_bias = jnp.sum(delta_pre.astype(jnp.float32), axis=0)
    delta_inner = matmul(delta_pre, up_matrix)
    return (delta_up, delta_up_bias, delta_down, delta_inner)


def local(
    hidden_in,
    lengths,
    cotangent,
    in_weight,
    in_bias,
    out_weight,
    out_bias,
    up_weight,
    up_bias,
    down_weight,
    down_bias,
    first_gain,
    first_shift,
    second_gain,
    second_shift,
):
    slot_count, token_count, width = hidden_in.shape
    seq_count = lax.axis_size("seq")
    seq_index = lax.axis_index("seq")
    length_full = token_count * seq_count
    row_count = slot_count * token_count
    (
        in_matrix,
        in_offset,
        out_matrix,
        out_offset,
        gain_one,
        shift_one,
        gain_two,
        shift_two,
        down_offset,
    ) = (
        lax.all_gather(in_weight, ("fsdp", "seq"), axis=0, tiled=True),
        lax.all_gather(in_bias, ("fsdp", "seq"), axis=0, tiled=True),
        lax.all_gather(out_weight, ("fsdp", "seq"), axis=0, tiled=True),
        lax.all_gather(out_bias, ("fsdp", "seq"), axis=0, tiled=True),
        lax.all_gather(first_gain, ("fsdp", "seq"), axis=0, tiled=True),
        lax.all_gather(first_shift, ("fsdp", "seq"), axis=0, tiled=True),
        lax.all_gather(second_gain, ("fsdp", "seq"), axis=0, tiled=True),
        lax.all_gather(second_shift, ("fsdp", "seq"), axis=0, tiled=True),
        lax.all_gather(down_bias, ("fsdp", "seq"), axis=0, tiled=True),
    )
    positions = seq_index * token_count + jnp.arange(token_count, dtype=jnp.int32)
    keep_local = positions[None, :] < lengths[:, None]
    keep_full = jnp.arange(length_full, dtype=jnp.int32)[None, :] < lengths[:, None]
    source = hidden_in.astype(jnp.float32)
    normed_one, pull_one = jax.vjp(
        layer_norm, source, gain_one.astype(jnp.float32), shift_one.astype(jnp.float32)
    )
    first_in = normed_one.astype(jnp.bfloat16).reshape(row_count, width)
    cosine_table, sine_table = rotary_tables(positions)
    joined = matmul(first_in, in_matrix) + in_offset.astype(jnp.float32)
    joined = joined.reshape(slot_count, token_count, 3, HEADS, HEAD_DIM)

    def rotate_both(query_part, key_part):
        return (
            rotate(query_part, cosine_table, sine_table),
            rotate(key_part, cosine_table, sine_table),
        )

    turned, pull_turn = jax.vjp(rotate_both, joined[:, :, 0], joined[:, :, 1])
    query, key_rows, value_rows = (
        lax.all_to_all(
            turned[0].astype(jnp.bfloat16), "seq", split_axis=2, concat_axis=1, tiled=True
        ),
        lax.all_to_all(
            turned[1].astype(jnp.bfloat16), "seq", split_axis=2, concat_axis=1, tiled=True
        ),
        lax.all_to_all(
            joined[:, :, 2].astype(jnp.bfloat16), "seq", split_axis=2, concat_axis=1, tiled=True
        ),
    )
    mixed_heads, log_sums = jax.vmap(attend_slot)(query, key_rows, value_rows, keep_full)
    mixed = lax.all_to_all(
        mixed_heads.astype(jnp.bfloat16), "seq", split_axis=1, concat_axis=2, tiled=True
    ).reshape(row_count, width)
    attn_branch = matmul(mixed, out_matrix) + out_offset.astype(jnp.float32)
    normed_two, pull_two = jax.vjp(
        layer_norm, source, gain_two.astype(jnp.float32), shift_two.astype(jnp.float32)
    )
    second_in = normed_two.astype(jnp.bfloat16)
    delta_out = jnp.where(keep_local[..., None], cotangent.astype(jnp.float32), 0.0)
    delta_low = delta_out.astype(jnp.bfloat16)
    delta_rows = delta_low.reshape(row_count, width)
    up_matrix, up_offset, down_matrix = (
        lax.all_gather(up_weight, "fsdp", axis=0, tiled=True),
        lax.all_gather(up_bias, "fsdp", axis=0, tiled=True),
        lax.all_gather(down_weight, "fsdp", axis=0, tiled=True),
    )
    inner_in = lax.all_gather(second_in, "seq", axis=1, tiled=True).reshape(
        slot_count * length_full, width
    )
    hidden_low, pull_act, branch_part = feed_forward(inner_in, up_matrix, up_offset, down_matrix)
    branch_sum = lax.psum_scatter(
        branch_part.reshape(slot_count, length_full, width).astype(jnp.bfloat16),
        "seq",
        scatter_dimension=1,
        tiled=True,
    ).astype(jnp.float32)
    mlp_branch = branch_sum + down_offset.astype(jnp.float32)
    delta_all = lax.all_gather(delta_low, "seq", axis=1, tiled=True).reshape(
        slot_count * length_full, width
    )
    delta_up, delta_up_bias, delta_down, delta_inner = feed_back(
        inner_in, hidden_low, pull_act, delta_all, up_matrix, down_matrix
    )
    second_delta = lax.psum_scatter(
        delta_inner.reshape(slot_count, length_full, width).astype(jnp.bfloat16),
        "seq",
        scatter_dimension=1,
        tiled=True,
    ).astype(jnp.float32)
    up_gradient, up_bias_gradient, down_gradient = (
        lax.psum_scatter(
            delta_up.astype(jnp.bfloat16), "fsdp", scatter_dimension=0, tiled=True
        ).astype(jnp.float32),
        lax.psum_scatter(
            delta_up_bias.astype(jnp.bfloat16), "fsdp", scatter_dimension=0, tiled=True
        ).astype(jnp.float32),
        lax.psum_scatter(
            delta_down.astype(jnp.bfloat16), "fsdp", scatter_dimension=0, tiled=True
        ).astype(jnp.float32),
    )
    layer_output = jnp.where(
        keep_local[..., None],
        source + attn_branch.reshape(slot_count, token_count, width) + mlp_branch,
        0.0,
    )
    source_two, gain_two_delta, shift_two_delta = pull_two(second_delta)
    bias_sum = jnp.sum(delta_out.reshape(row_count, width), axis=0)
    out_delta = transposed_times(mixed, delta_rows)
    mixed_delta = times_transposed(delta_rows, out_matrix).astype(jnp.bfloat16)
    mixed_delta = lax.all_to_all(
        mixed_delta.reshape(slot_count, token_count, HEADS, HEAD_DIM),
        "seq",
        split_axis=2,
        concat_axis=1,
        tiled=True,
    )
    query_delta, key_delta, value_delta = jax.vmap(attend_slot_back)(
        query, key_rows, value_rows, keep_full, log_sums, mixed_delta
    )
    query_back, key_back, value_back = (
        lax.all_to_all(
            query_delta.astype(jnp.bfloat16), "seq", split_axis=1, concat_axis=2, tiled=True
        ),
        lax.all_to_all(
            key_delta.astype(jnp.bfloat16), "seq", split_axis=1, concat_axis=2, tiled=True
        ),
        lax.all_to_all(
            value_delta.astype(jnp.bfloat16), "seq", split_axis=1, concat_axis=2, tiled=True
        ),
    )
    query_plain, key_plain = pull_turn(
        (query_back.astype(jnp.float32), key_back.astype(jnp.float32))
    )
    joined_delta = jnp.stack([query_plain, key_plain, value_back.astype(jnp.float32)], axis=2)
    joined_delta = joined_delta.reshape(row_count, 3 * width).astype(jnp.bfloat16)
    in_delta = transposed_times(first_in, joined_delta)
    in_bias_delta = jnp.sum(joined_delta.astype(jnp.float32), axis=0)
    first_delta = times_transposed(joined_delta, in_matrix).reshape(slot_count, token_count, width)
    source_one, gain_one_delta, shift_one_delta = pull_one(first_delta)
    (
        in_gradient,
        in_bias_gradient,
        out_gradient,
        bias_gradient,
        gain_one_gradient,
        shift_one_gradient,
        gain_two_gradient,
        shift_two_gradient,
    ) = (
        lax.psum_scatter(in_delta, ("fsdp", "seq"), scatter_dimension=0, tiled=True),
        lax.psum_scatter(in_bias_delta, ("fsdp", "seq"), scatter_dimension=0, tiled=True),
        lax.psum_scatter(out_delta, ("fsdp", "seq"), scatter_dimension=0, tiled=True),
        lax.psum_scatter(bias_sum, ("fsdp", "seq"), scatter_dimension=0, tiled=True),
        lax.psum_scatter(gain_one_delta, ("fsdp", "seq"), scatter_dimension=0, tiled=True),
        lax.psum_scatter(shift_one_delta, ("fsdp", "seq"), scatter_dimension=0, tiled=True),
        lax.psum_scatter(gain_two_delta, ("fsdp", "seq"), scatter_dimension=0, tiled=True),
        lax.psum_scatter(shift_two_delta, ("fsdp", "seq"), scatter_dimension=0, tiled=True),
    )
    input_gradient = delta_out + source_one + source_two
    return (
        layer_output,
        input_gradient,
        in_gradient,
        in_bias_gradient,
        out_gradient,
        bias_gradient,
        up_gradient,
        up_bias_gradient,
        down_gradient,
        bias_gradient,
        gain_one_gradient,
        shift_one_gradient,
        gain_two_gradient,
        shift_two_gradient,
    )


def solution(mesh):
    return jax.shard_map(
        local,
        mesh=mesh,
        in_specs=(
            P("fsdp", "seq", None),
            P("fsdp"),
            P("fsdp", "seq", None),
            P(("fsdp", "seq"), None),
            P(("fsdp", "seq")),
            P(("fsdp", "seq"), None),
            P(("fsdp", "seq")),
            P(("fsdp", "seq"), None),
            P(("fsdp", "seq")),
            P(("fsdp", "seq"), None),
            P(("fsdp", "seq")),
            P(("fsdp", "seq")),
            P(("fsdp", "seq")),
            P(("fsdp", "seq")),
            P(("fsdp", "seq")),
        ),
        out_specs=(
            P("fsdp", "seq", None),
            P("fsdp", "seq", None),
            P(("fsdp", "seq"), None),
            P(("fsdp", "seq")),
            P(("fsdp", "seq"), None),
            P(("fsdp", "seq")),
            P(("fsdp", "seq"), None),
            P(("fsdp", "seq")),
            P(("fsdp", "seq"), None),
            P(("fsdp", "seq")),
            P(("fsdp", "seq")),
            P(("fsdp", "seq")),
            P(("fsdp", "seq")),
            P(("fsdp", "seq")),
        ),
        check_vma=False,
    )
```

profile of v0, /device:TPU:0, one launch (start us, length us, event | category | flops | bytes accessed | tf_op | source)
XLA Modules:
  0.0 1959.2 jit_solution(5670677345125691977)
XLA Ops:
  16.4 43.3 %all-reduce.25 = (bf16[6144]{0:T(1024)(128)(2,1)S(1)}, bf16[2048]{0:T(1024)(128)(2,1)S(1)}, bf16[2048]{0:T(1024)(128)(2,1)S(1)}, bf16[2048]{0:T(1024)(128)(2,1)S...) all-reduce(bf16[6144]{0:T(1024)(128)(2,1)S(1)} %dynamic-update-slic, ...), channel_id=1, replica_groups=mesh['fsdp'=8,'seq'=4] {'fsdp','seq'}, use_global_device_ids=true, to_apply=%add.12 | all-reduce | flops 18432 | bytes 73728
  67.0 9.8 all-gather
  76.8 66.3 %all-gather.12.cloned.1.call-done = bf16[1,1024,2048]{2,1,0:T(8,128)(2,1)} async-done(((bf16[1,256,2048]{2,1,0:T(8,128)(2,1)}), bf16[1,1024,2048]{2,1,0:T(8,128)(2,1)}) %all-gather.12.cloned.1.call-update) | async-done | bytes 4194320 | tf_op jit(solution)/shard_map/all_gather | solution.py:243
  143.0 54.8 %all-gather.14.cloned.1.call-done = bf16[2048,2048]{1,0:T(8,128)(2,1)} async-done(((bf16[256,2048]{1,0:T(8,128)(2,1)}), bf16[2048,2048]{1,0:T(8,128)(2,1)}) %all-gather.14.cloned.1.call-update) | async-done | bytes 8388624 | tf_op jit(solution)/shard_map/all_gather | solution.py:239
  197.9 31.6 %multiply_convert_fusion.1 = (bf16[1024,2048]{1,0:T(8,128)(2,1)}, f32[1024,2048]{1,0:T(8,128)}, f32[1024,2048]{1,0:T(8,128)}) fusion(f32[2048]{0:T(1024)S(1)} %bitcast.299, bf16[2048,2048]{1,0:T(8,128)(2,1)} %all-gather.14.cloned.1.call-done, bf16[1,1024,2048]{2,1,0:T(8,128)(2,1)} %all-gather.12.cloned.1.call-done), kind=kOutput, calls=%fused_computation.61 | convolution fusion | flops 8728346624 | bytes 33562624 | tf_op jit(solution)/shard_map/dot_general | solution.py:44
  229.5 50.8 %all-gather.18.cloned.1.call-done = bf16[1,1024,2048]{2,1,0:T(8,128)(2,1)} async-done(((bf16[1,256,2048]{2,1,0:T(8,128)(2,1)}), bf16[1,1024,2048]{2,1,0:T(8,128)(2,1)}) %all-gather.18.cloned.1.call-update) | async-done | bytes 4194320 | tf_op jit(solution)/shard_map/all_gather | solution.py:254
  280.3 54.7 %all-gather.16.cloned.1.call-done = bf16[2048,2048]{1,0:T(8,128)(2,1)} async-done(((bf16[256,2048]{1,0:T(8,128)(2,1)}), bf16[2048,2048]{1,0:T(8,128)(2,1)}) %all-gather.16.cloned.1.call-update) | async-done | bytes 8388624 | tf_op jit(solution)/shard_map/all_gather | solution.py:241
  335.0 19.4 fusion.110
  356.3 12.9 convert_bitcast_fusion
  369.3 14.1 convolution_convert_fusion.1
  383.9 31.2 %all-gather.10.cloned.1.call-done = bf16[2048,2048]{1,0:T(8,128)(2,1)} async-done(((bf16[64,2048]{1,0:T(8,128)(2,1)}), bf16[2048,2048]{1,0:T(8,128)(2,1)}) %all-gather.10.cloned.1.call-update) | async-done | bytes 8388624 | tf_op jit(solution)/shard_map/all_gather | solution.py:188
  415.0 5.7 fusion.88
  427.0 163.5 %all-gather.8.cloned.1.call-done = bf16[2048,6144]{1,0:T(8,128)(2,1)} async-done(((bf16[64,6144]{1,0:T(8,128)(2,1)}), bf16[2048,6144]{1,0:T(8,128)(2,1)}) %all-gather.8.cloned.1.call-update) | async-done | bytes 25165840 | tf_op jit(solution)/shard_map/all_gather | solution.py:186
  590.5 12.6 fusion.68
  618.9 53.1 %all-to-all-done.1 = bf16[1,256,16,128]{3,1,0,2:T(8,128)(2,1)} async-done(((bf16[1,256,16,128]{3,1,0,2:T(8,128)(2,1)}), bf16[1,256,16,128]{3,1,0,2:T(8,128)(2,1)}, u32[]{:S(2)}, u32[]{:S(2)}) %all-to-all-start.1) | async-done | bytes 1048608 | tf_op jit(solution)/shard_map/all_to_all | solution.py:219
  679.0 33.3 %all-to-all-done = bf16[1,256,16,128]{3,1,0,2:T(8,128)(2,1)S(1)} async-done(((bf16[1,256,16,128]{3,1,0,2:T(8,128)(2,1)}), bf16[1,256,16,128]{3,1,0,2:T(8,128)(2,1)S(1)}, u32[]{:S(2)}, u32[]{:S(2)}) %all-to-all-start) | async-done | bytes 1048608 | tf_op jit(solution)/shard_map/all_to_all | solution.py:216
  716.6 15.0 convolution_convert_fusion
  745.4 26.7 %while.31 = (s32[]{:T(128)}, bf16[2,1,512,4,128]{4,2,0,3,1:T(8,128)(2,1)}, f32[2,1,4,512]{3,2,1,0:T(4,128)S(1)}, s32[2]{0:T(128)S(1)}, bf16[1,1024,4,128]{3,1,2,...) while((s32[]{:T(128)}, ...), condition=%wide.region_5.6_spmd.clone, body=%wide.region_2.5_spmd.clone.sunk | while | flops 1099955712 | bytes 35199700 | solution.py:81
  773.2 55.0 %while.32 = (s32[]{:T(128)}, f32[1,1024,4,128]{1,3,2,0:T(8,128)S(1)}, f32[1,1024,4,128]{1,3,2,0:T(8,128)}, bf16[2,1,512,4,128]{4,2,0,3,1:T(8,128)(2,1)}, s32[2]{...) while((s32[]{:T(128)}, ...), condition=%wide.region_9.10_spmd.clone, body=%wide.region_7.9_spmd.clone.sunk | while | flops 2709257728 | bytes 170966912 | solution.py:131
  836.5 22.4 %all-to-all-done.5 = bf16[1,1024,4,128]{3,2,0,1:T(4,128)(2,1)S(1)} async-done(((bf16[1,1024,4,128]{3,2,0,1:T(4,128)(2,1)}), bf16[1,1024,4,128]{3,2,0,1:T(4,128)(2,1)S(1)}, u32[]{:S(2)}, u32[]{:S(2)}) %all-to-all-start.5) | async-done | bytes 1048608 | tf_op jit(solution)/shard_map/all_to_all | solution.py:297
  863.5 14.3 convert_bitcast_fusion.1
  880.6 8.0 all-to-all-done.6
  900.6 45.7 %all-to-all-done.7 = bf16[1,1024,4,128]{3,2,0,1:T(4,128)(2,1)} async-done(((bf16[1,1024,4,128]{3,2,0,1:T(4,128)(2,1)}), bf16[1,1024,4,128]{3,2,0,1:T(4,128)(2,1)}, u32[]{:S(2)}, u32[]{:S(2)}) %all-to-all-start.7) | async-done | bytes 1048608 | tf_op jit(solution)/shard_map/all_to_all | solution.py:303
  966.1 31.0 %all-to-all-done.3 = bf16[1,1024,4,128]{3,2,0,1:T(4,128)(2,1)S(1)} async-done(((bf16[1,1024,4,128]{3,2,0,1:T(4,128)(2,1)}), bf16[1,1024,4,128]{3,2,0,1:T(4,128)(2,1)S(1)}, u32[]{:S(2)}, u32[]{:S(2)}) %all-to-all-start.3) | async-done | bytes 1048608 | tf_op jit(solution)/shard_map/all_to_all | solution.py:227
  999.8 14.7 fusion.79
  1024.3 8.1 fusion.94
  1033.1 21.9 %fusion.103 = f32[2048,6144]{1,0:T(8,128)} fusion(bf16[256,6144]{0,1:T(8,128)(2,1)} %bitcast.282, bf16[1,256,2048]{2,1,0:T(8,128)(2,1)S(1)} %copy-done.4, f32[2048]{0:T(1024)S(1)} %copy-done.31, f32[2048]{0:T(1024)S(1)} %copy-done.29, f32[256]{0:T(256)S(1)} %copy-done.35, f32[256]{0:T(256)S(1)} %copy-done.37), kind=kOutput, calls=%fused_computation.179 | convolution fusion | flops 6445596672 | bytes 54544384 | tf_op jit(solution)/shard_map/dot_general | solution.py:50
  1056.9 13.9 all-reduce.19
  1077.1 7.5 fusion.71
  1084.6 62.8 %all-reduce.28.cloned.1.call-done = (f32[6144]{0:T(1024)}, f32[2048]{0:T(1024)}, f32[2048]{0:T(1024)}, f32[2048]{0:T(1024)}, f32[2048]{0:T(1024)}, /*index=5*/f32[2048]{0:T(1024)}) async-done(((f32[6144]{0:T(1024)}, f32[2048]{0:T(1024)}, f32[2048]{0:T(1024)}, f32[2048]{0:T(1024)}, f32[2048]{0:T(1024)}, /*index=5*/f32[2048]{0:T(1024)}), (f32[6144]{0:T(1024)}, f32[2048]{0:T(1024)}, f32[2048]{0:T(1024)}, ...) | async-done | bytes 65552
  1154.5 361.0 %reduce-scatter.13.cloned.1.call-done = f32[64,2048]{1,0:T(8,128)} async-done(((f32[2048,2048]{1,0:T(8,128)}), f32[64,2048]{1,0:T(8,128)}) %reduce-scatter.13.cloned.1.call-update) | async-done | bytes 524304 | tf_op jit(solution)/shard_map/reduce_scatter | solution.py:328
  1515.5 436.4 %reduce-scatter.11.cloned.1.call-done = f32[64,6144]{1,0:T(8,128)} async-done(((f32[2048,6144]{1,0:T(8,128)}), f32[64,6144]{1,0:T(8,128)}) %reduce-scatter.11.cloned.1.call-update) | async-done | bytes 1572880 | tf_op jit(solution)/shard_map/reduce_scatter | solution.py:326
  (291 shorter events, 215.2 us)
Async XLA Ops:
  7.2 135.9 %all-gather.12.cloned.1.call-start = ((), (), s32[]{:S(2)}) async-start(), calls=%async_computation.16 | async-start | bytes 5242880 | tf_op jit(solution)/shard_map/all_gather | solution.py:243
  7.2 56.6 %copy-start.18 = (bf16[1,256,2048]{2,1,0:T(8,128)(2,1)S(1)}, bf16[1,256,2048]{2,1,0:T(8,128)(2,1)}, u32[]{:S(2)}) copy-start(bf16[1,256,2048]{2,1,0:T(8,128)(2,1)} %param.21) | copy-start | bytes 3145732
  8.8 581.7 %copy-start.36 = (f32[256]{0:T(256)}, f32[256]{0:T(256)S(1)}, u32[]{:S(2)}) copy-start(f32[256]{0:T(256)S(1)} %broadcast_multiply_fusion.1) | copy-start | bytes 3076
  10.4 49.2 %copy-start.38 = (f32[256]{0:T(256)}, f32[256]{0:T(256)S(1)}, u32[]{:S(2)}) copy-start(f32[256]{0:T(256)S(1)} %fusion.78) | copy-start | bytes 3076
  10.5 580.0 %copy-start.34 = (f32[256]{0:T(256)}, f32[256]{0:T(256)S(1)}, u32[]{:S(2)}) copy-start(f32[256]{0:T(256)S(1)} %fusion.101) | copy-start | bytes 3076
  62.4 135.5 %all-gather.14.cloned.1.call-start = ((), (), s32[]{:S(2)}) async-start(), calls=%async_computation.17 | async-start | bytes 9437184 | tf_op jit(solution)/shard_map/all_gather | solution.py:239
  63.1 217.1 %all-gather.18.cloned.1.call-start = ((), (), s32[]{:S(2)}) async-start(), calls=%async_computation.20 | async-start | bytes 5242880 | tf_op jit(solution)/shard_map/all_gather | solution.py:254
  65.1 269.8 %all-gather.16.cloned.1.call-start = ((), (), s32[]{:S(2)}) async-start(), calls=%async_computation.18 | async-start | bytes 9437184 | tf_op jit(solution)/shard_map/all_gather | solution.py:241
  65.7 349.3 %all-gather.10.cloned.1.call-start = ((), (), s32[]{:S(2)}) async-start(), calls=%async_computation.15 | async-start | bytes 8650752 | tf_op jit(solution)/shard_map/all_gather | solution.py:188
  66.3 524.2 %all-gather.8.cloned.1.call-start = ((), (), s32[]{:S(2)}) async-start(), calls=%async_computation.14 | async-start | bytes 25952256 | tf_op jit(solution)/shard_map/all_gather | solution.py:186
  66.9 932.8 %reduce-scatter.9.cloned.1.call-start = ((), (), s32[]{:S(2)}) async-start(), calls=%async_computation.21 | async-start | bytes 5242880 | tf_op jit(solution)/shard_map/reduce_scatter | solution.py:260
  369.2 702.3 %reduce-scatter.15.cloned.1.call-start = ((), (), s32[]{:S(2)}) async-start(), calls=%async_computation.24 | async-start | bytes 9437184 | tf_op jit(solution)/shard_map/reduce_scatter | solution.py:267
  383.4 207.1 %copy-start.28 = (f32[2048]{0:T(1024)}, f32[2048]{0:T(1024)S(1)}, u32[]{:S(2)}) copy-start(f32[2048]{0:T(1024)S(1)} %convert_element_type.269) | copy-start | bytes 24580
  383.5 207.1 %copy-start.30 = (f32[2048]{0:T(1024)}, f32[2048]{0:T(1024)S(1)}, u32[]{:S(2)}) copy-start(f32[2048]{0:T(1024)S(1)} %convert_element_type.270) | copy-start | bytes 24580
  383.8 226.1 %copy-start.24 = (f32[256,32]{1,0:T(8,128)}, f32[256,32]{1,0:T(8,128)S(1)}, u32[]{:S(2)}) copy-start(f32[256,32]{1,0:T(8,128)S(1)} %copy.133) | copy-start | bytes 98308
  383.9 226.1 %copy-start.26 = (f32[256,32]{1,0:T(8,128)}, f32[256,32]{1,0:T(8,128)S(1)}, u32[]{:S(2)}) copy-start(f32[256,32]{1,0:T(8,128)S(1)} %copy.134) | copy-start | bytes 98308
  420.8 169.7 %copy-start.3 = (bf16[1,256,2048]{2,1,0:T(8,128)(2,1)S(1)}, bf16[1,256,2048]{2,1,0:T(8,128)(2,1)}, u32[]{:S(2)}) copy-start(bf16[1,256,2048]{2,1,0:T(8,128)(2,1)} %param.19) | copy-start | bytes 3145732
  422.3 190.5 %all-to-all-start.4 = ((bf16[1,256,16,128]{3,1,0,2:T(8,128)(2,1)}), bf16[1,256,16,128]{3,1,0,2:T(8,128)(2,1)}, u32[]{:S(2)}, u32[]{:S(2)}) async-start(bf16[1,256,16,128]{3,1,0,2:T(8,128)(2,1)} %copy.146), calls=%async_computation.5 | async-start | bytes 2097152 | tf_op jit(solution)/shard_map/all_to_all | solution.py:286
  612.8 59.3 %all-to-all-start.1 = ((bf16[1,256,16,128]{3,1,0,2:T(8,128)(2,1)}), bf16[1,256,16,128]{3,1,0,2:T(8,128)(2,1)}, u32[]{:S(2)}, u32[]{:S(2)}) async-start(bf16[1,256,16,128]{3,1,0,2:T(8,128)(2,1)} %maximum_bitcast_fusion.1), calls=%async_computation.1 | async-start | bytes 2097152 | tf_op jit(solution)/shard_map/all_to_all | solution.py:219
  672.0 40.2 %all-to-all-start = ((bf16[1,256,16,128]{3,1,0,2:T(8,128)(2,1)}), bf16[1,256,16,128]{3,1,0,2:T(8,128)(2,1)S(1)}, u32[]{:S(2)}, u32[]{:S(2)}) async-start(bf16[1,256,16,128]{3,1,0,2:T(8,128)(2,1)} %maximum_bitcast_fusion), calls=%async_computation | async-start | bytes 2097152 | tf_op jit(solution)/shard_map/all_to_all | solution.py:216
  712.3 29.8 %all-to-all-start.2 = ((bf16[1,256,16,128]{3,1,0,2:T(8,128)(2,1)}), bf16[1,256,16,128]{3,1,0,2:T(8,128)(2,1)}, u32[]{:S(2)}, u32[]{:S(2)}) async-start(bf16[1,256,16,128]{3,1,0,2:T(8,128)(2,1)} %bitcast.288), calls=%async_computation.2 | async-start | bytes 2097152 | tf_op jit(solution)/shard_map/all_to_all | solution.py:222
  716.5 357.7 %reduce-scatter.17.cloned.1.call-start = ((), (), s32[]{:S(2)}) async-start(), calls=%async_computation.25 | async-start | bytes 9437184 | tf_op jit(solution)/shard_map/reduce_scatter | solution.py:273
  831.3 27.6 %all-to-all-start.5 = ((bf16[1,1024,4,128]{3,2,0,1:T(4,128)(2,1)}), bf16[1,1024,4,128]{3,2,0,1:T(4,128)(2,1)S(1)}, u32[]{:S(2)}, u32[]{:S(2)}) async-start(bf16[1,1024,4,128]{3,2,0,1:T(4,128)(2,1)} %copy.149), calls=%async_computation.6 | async-start | bytes 2097152 | tf_op jit(solution)/shard_map/all_to_all | solution.py:297
  859.9 28.8 %all-to-all-start.6 = ((bf16[1,1024,4,128]{3,2,0,1:T(4,128)(2,1)}), bf16[1,1024,4,128]{3,2,0,1:T(4,128)(2,1)S(1)}, u32[]{:S(2)}, u32[]{:S(2)}) async-start(bf16[1,1024,4,128]{3,2,0,1:T(4,128)(2,1)} %copy.152), calls=%async_computation.7 | async-start | bytes 2097152 | tf_op jit(solution)/shard_map/all_to_all | solution.py:300
  863.4 213.6 %reduce-scatter.7.cloned.1.call-start = ((), (), s32[]{:S(2)}) async-start(), calls=%async_computation.19 | async-start | bytes 5242880 | tf_op jit(solution)/shard_map/reduce_scatter | solution.py:247
  888.6 57.6 %all-to-all-start.7 = ((bf16[1,1024,4,128]{3,2,0,1:T(4,128)(2,1)}), bf16[1,1024,4,128]{3,2,0,1:T(4,128)(2,1)}, u32[]{:S(2)}, u32[]{:S(2)}) async-start(bf16[1,1024,4,128]{3,2,0,1:T(4,128)(2,1)} %copy.154), calls=%async_computation.8 | async-start | bytes 2097152 | tf_op jit(solution)/shard_map/all_to_all | solution.py:303
  900.6 51.2 %copy-start.27 = (f32[256,32]{1,0:T(8,128)S(1)}, f32[256,32]{1,0:T(8,128)}, u32[]{:S(2)}) copy-start(f32[256,32]{1,0:T(8,128)} %copy-done.26) | copy-start | bytes 98308
  946.3 50.8 %all-to-all-start.3 = ((bf16[1,1024,4,128]{3,2,0,1:T(4,128)(2,1)}), bf16[1,1024,4,128]{3,2,0,1:T(4,128)(2,1)S(1)}, u32[]{:S(2)}, u32[]{:S(2)}) async-start(bf16[1,1024,4,128]{3,2,0,1:T(4,128)(2,1)} %copy.143), calls=%async_computation.3 | async-start | bytes 2097152 | tf_op jit(solution)/shard_map/all_to_all | solution.py:227
  950.2 197.1 %all-reduce.28.cloned.1.call-start = ((), (), s32[]{:S(2)}) async-start(), calls=%async_computation.26 | async-start | bytes 131072
  1024.2 491.2 %reduce-scatter.13.cloned.1.call-start = ((), (), s32[]{:S(2)}) async-start(), calls=%async_computation.23 | async-start | bytes 17301504 | tf_op jit(solution)/shard_map/reduce_scatter | solution.py:328
  1032.4 919.5 %reduce-scatter.11.cloned.1.call-start = ((), (), s32[]{:S(2)}) async-start(), calls=%async_computation.22 | async-start | bytes 51904512 | tf_op jit(solution)/shard_map/reduce_scatter | solution.py:326
  1148.1 804.3 %copy-start.47 = (f32[64]{0:T(128)}, f32[64]{0:T(128)S(1)}, u32[]{:S(2)}) copy-start(f32[64]{0:T(128)S(1)} %dynamic-slice.16) | copy-start | bytes 772
  (44 other events, 361.8 us)
Sparse Core Ops, SparseCore 0:
  62.5 80.5 all-gather.11
  144.9 52.9 all-gather.13
  199.5 80.7 all-gather.17
  282.0 52.9 all-gather.15
  337.7 77.2 all-gather.9
  417.8 172.6 all-gather.7
  592.8 99.6 reduce-scatter.8
  696.4 88.4 reduce-scatter.14
  788.3 71.2 reduce-scatter.16
  877.9 111.9 reduce-scatter.6
  1024.4 122.9 all-reduce.27
  1150.1 365.3 reduce-scatter.12
  1522.5 429.3 reduce-scatter.10
where the time goes:
time: 1960 us
  waiting for transfers between devices  1480 us (76%)
  matrix products  222 us (11%)
  local copies, waits for them, and re-layouts  76 us (4%)
  blocking collectives  66.9 us (3%)
  other arithmetic  53.9 us (3%)
  starting transfers between devices  32.8 us (2%)
    reduce_scatter x1, waiting for transfers between devices, local(): lax.psum_scatter(in_delta, ('fsdp', 'seq'), scatter_dimension=0, tiled=True)  436 us
    reduce_scatter x1, waiting for transfers between devices, local(): lax.psum_scatter(out_delta, ('fsdp', 'seq'), scatter_dimension=0, tiled=T...  361 us
    all_gather x1, waiting for transfers between devices, local(): lax.all_gather(in_weight, ('fsdp', 'seq'), axis=0, tiled=True)  164 us
    dot_general x4, matrix products, times_transposed(): lax.dot_general(left_side, right_side, (((1,), (1,)), ((), ())), preferre...  71.4 us
    all_gather x1, waiting for transfers between devices, local(): lax.all_gather(second_in, 'seq', axis=1, tiled=True)  66.3 us
    unnamed x14, waiting for transfers between devices  65.2 us
    dot_general x4, matrix products, transposed_times(): lax.dot_general(left_side, right_side, (((0,), (0,)), ((), ())), preferre...  59.1 us
    unnamed x2, blocking collectives  57.1 us
  transfers between devices with their start and end apart: 21, of which 16 were waited for; matrix products, arithmetic and copies ran while one was open for 16% of the time, Pallas kernels for 0%

commit v1 on v0

--- a/solution.py
+++ b/solution.py
@@ -8,6 +8,18 @@
 ROT = 32
 EPSILON = 1e-05
 MASKED_SCORE = -1e30
+
+
+def serve_the_task(row_data, dim_i, z):
+    all_rows, carry = (row_data.shape[:dim_i], row_data.shape[dim_i + 1 :])
+    state_now = row_data.reshape(*all_rows, z, -1, *carry)
+    return jnp.moveaxis(state_now, dim_i, 0)
+
+
+def clear_the_words(body, row_dim):
+    body = jnp.moveaxis(body, 0, row_dim)
+    then = body.shape
+    return body.reshape(*then[:row_dim], then[row_dim] * then[row_dim + 1], *then[row_dim + 2 :])
 
 
 def layer_norm(values, norm_gain, norm_shift):
@@ -167,6 +179,21 @@
     second_gain,
     second_shift,
 ):
+
+    def _draw_stages_all(x_in, axis_id, view, chunk):
+        taken_in = lax.axis_size(axis_id)
+        current_arr = lax.axis_index(axis_id)
+        reply, f_now = (taken_in, current_arr)
+        placed = serve_the_task(x_in, view, reply)
+        slots = [placed[f_now]]
+        for num in [*range(1, reply)]:
+            m_next = placed[f_now ^ num]
+            d_next = lax.ppermute(m_next, axis_id, [(d, d ^ num) for d in range(reply)])
+            slots.append(d_next)
+        seen_now = jnp.stack(slots)
+        placed = seen_now[f_now ^ jnp.arange(reply)]
+        return clear_the_words(placed, chunk)
+
     slot_count, token_count, width = hidden_in.shape
     seq_count = lax.axis_size("seq")
     seq_index = lax.axis_index("seq")
@@ -216,9 +243,7 @@
         lax.all_to_all(
             turned[0].astype(jnp.bfloat16), "seq", split_axis=2, concat_axis=1, tiled=True
         ),
-        lax.all_to_all(
-            turned[1].astype(jnp.bfloat16), "seq", split_axis=2, concat_axis=1, tiled=True
-        ),
+        _draw_stages_all(turned[1].astype(jnp.bfloat16), "seq", 2, 1),
         lax.all_to_all(
             joined[:, :, 2].astype(jnp.bfloat16), "seq", split_axis=2, concat_axis=1, tiled=True
         ),

time: 1960 us -> 1960 us (level)
    all_to_all x1 -> x0, waiting for transfers between devices: 53.1 us -> none  [local(): lax.all_to_all(turned[1].astype(jnp.bfloat16), 'seq', split_axis=2, conca...]
  transfers between devices with their start and end apart: 21 -> 23, of which waited for: 16 -> 16; matrix products, arithmetic and copies ran while one was open for 16% -> 17% of each run, Pallas kernels for 0% -> 0%
where the time goes in v1:
time: 1960 us; the launch traced here: 1950 us
  waiting for transfers between devices  1470 us (75%)
  matrix products  222 us (11%)
  local copies, waits for them, and re-layouts  82 us (4%)
  blocking collectives  66.9 us (3%)
  other arithmetic  55.1 us (3%)
  starting transfers between devices  34.2 us (2%)
    reduce_scatter x1, waiting for transfers between devices, local(): lax.psum_scatter(in_delta, ('fsdp', 'seq'), scatter_dimension=0, tiled=True)  437 us
    reduce_scatter x1, waiting for transfers between devices, local(): lax.psum_scatter(out_delta, ('fsdp', 'seq'), scatter_dimension=0, tiled=T...  361 us
    all_gather x1, waiting for transfers between devices, local(): lax.all_gather(in_weight, ('fsdp', 'seq'), axis=0, tiled=True)  164 us
    dot_general x4, matrix products, times_transposed(): lax.dot_general(left_side, right_side, (((1,), (1,)), ((), ())), preferre...  71.4 us
    all_gather x1, waiting for transfers between devices, local(): lax.all_gather(second_in, 'seq', axis=1, tiled=True)  66.3 us
    unnamed x14, waiting for transfers between devices  63.3 us
    dot_general x4, matrix products, transposed_times(): lax.dot_general(left_side, right_side, (((0,), (0,)), ((), ())), preferre...  58.4 us
    unnamed x2, blocking collectives  57.2 us
  transfers between devices with their start and end apart: 23, of which 16 were waited for; matrix products, arithmetic and copies ran while one was open for 17% of the time, Pallas kernels for 0%

profile of v1, /device:TPU:0, one launch (start us, length us, event | category | flops | bytes accessed | tf_op | source)
XLA Modules:
  0.0 1954.5 jit_solution(7566001488589176065)
XLA Ops:
  16.4 43.2 %all-reduce.25 = (bf16[6144]{0:T(1024)(128)(2,1)S(1)}, bf16[2048]{0:T(1024)(128)(2,1)S(1)}, bf16[2048]{0:T(1024)(128)(2,1)S(1)}, bf16[2048]{0:T(1024)(128)(2,1)S...) all-reduce(bf16[6144]{0:T(1024)(128)(2,1)S(1)} %dynamic-update-slic, ...), channel_id=1, replica_groups=mesh['fsdp'=8,'seq'=4] {'fsdp','seq'}, use_global_device_ids=true, to_apply=%add.12 | all-reduce | flops 18432 | bytes 73728
  67.0 9.8 all-gather
  76.7 66.3 %all-gather.12.cloned.1.call-done = bf16[1,1024,2048]{2,1,0:T(8,128)(2,1)} async-done(((bf16[1,256,2048]{2,1,0:T(8,128)(2,1)}), bf16[1,1024,2048]{2,1,0:T(8,128)(2,1)}) %all-gather.12.cloned.1.call-update) | async-done | bytes 4194320 | tf_op jit(solution)/shard_map/all_gather | solution.py:268
  143.0 54.8 %all-gather.14.cloned.1.call-done = bf16[2048,2048]{1,0:T(8,128)(2,1)} async-done(((bf16[256,2048]{1,0:T(8,128)(2,1)}), bf16[2048,2048]{1,0:T(8,128)(2,1)}) %all-gather.14.cloned.1.call-update) | async-done | bytes 8388624 | tf_op jit(solution)/shard_map/all_gather | solution.py:264
  197.9 31.6 %multiply_convert_fusion.1 = (bf16[1024,2048]{1,0:T(8,128)(2,1)}, f32[1024,2048]{1,0:T(8,128)}, f32[1024,2048]{1,0:T(8,128)}) fusion(f32[2048]{0:T(1024)S(1)} %bitcast.314, bf16[2048,2048]{1,0:T(8,128)(2,1)} %all-gather.14.cloned.1.call-done, bf16[1,1024,2048]{2,1,0:T(8,128)(2,1)} %all-gather.12.cloned.1.call-done), kind=kOutput, calls=%fused_computation.62 | convolution fusion | flops 8728346624 | bytes 33562624 | tf_op jit(solution)/shard_map/dot_general | solution.py:56
  229.4 50.8 %all-gather.18.cloned.1.call-done = bf16[1,1024,2048]{2,1,0:T(8,128)(2,1)} async-done(((bf16[1,256,2048]{2,1,0:T(8,128)(2,1)}), bf16[1,1024,2048]{2,1,0:T(8,128)(2,1)}) %all-gather.18.cloned.1.call-update) | async-done | bytes 4194320 | tf_op jit(solution)/shard_map/all_gather | solution.py:279
  280.3 54.7 %all-gather.16.cloned.1.call-done = bf16[2048,2048]{1,0:T(8,128)(2,1)} async-done(((bf16[256,2048]{1,0:T(8,128)(2,1)}), bf16[2048,2048]{1,0:T(8,128)(2,1)}) %all-gather.16.cloned.1.call-update) | async-done | bytes 8388624 | tf_op jit(solution)/shard_map/all_gather | solution.py:266
  335.0 19.4 fusion.119
  356.3 12.9 convert_bitcast_fusion
  369.2 14.1 convolution_convert_fusion.1
  383.8 31.2 %all-gather.10.cloned.1.call-done = bf16[2048,2048]{1,0:T(8,128)(2,1)} async-done(((bf16[64,2048]{1,0:T(8,128)(2,1)}), bf16[2048,2048]{1,0:T(8,128)(2,1)}) %all-gather.10.cloned.1.call-update) | async-done | bytes 8388624 | tf_op jit(solution)/shard_map/all_gather | solution.py:215
  426.9 163.6 %all-gather.8.cloned.1.call-done = bf16[2048,6144]{1,0:T(8,128)(2,1)} async-done(((bf16[64,6144]{1,0:T(8,128)(2,1)}), bf16[2048,6144]{1,0:T(8,128)(2,1)}) %all-gather.8.cloned.1.call-update) | async-done | bytes 25165840 | tf_op jit(solution)/shard_map/all_gather | solution.py:213
  590.5 12.6 fusion.68
  628.0 38.7 %all-to-all-done = bf16[1,256,16,128]{3,1,0,2:T(8,128)(2,1)} async-done(((bf16[1,256,16,128]{3,1,0,2:T(8,128)(2,1)}), bf16[1,256,16,128]{3,1,0,2:T(8,128)(2,1)}, u32[]{:S(2)}, u32[]{:S(2)}) %all-to-all-start) | async-done | bytes 1048608 | tf_op jit(solution)/shard_map/all_to_all | solution.py:243
  672.3 14.3 convolution_convert_fusion
  688.9 14.3 collective-permute-done.1
  710.5 24.4 %all-to-all-done.1 = bf16[1,256,16,128]{3,1,0,2:T(8,128)(2,1)} async-done(((bf16[1,256,16,128]{3,1,0,2:T(8,128)(2,1)}), bf16[1,256,16,128]{3,1,0,2:T(8,128)(2,1)}, u32[]{:S(2)}, u32[]{:S(2)}) %all-to-all-start.1) | async-done | bytes 1048608 | tf_op jit(solution)/shard_map/all_to_all | solution.py:247
  738.2 26.9 %while.31 = (s32[]{:T(128)}, bf16[2,1,512,4,128]{4,2,0,3,1:T(8,128)(2,1)}, f32[2,1,4,512]{3,2,1,0:T(4,128)S(1)}, s32[2]{0:T(128)S(1)}, bf16[1,1024,4,128]{3,1,2,...) while((s32[]{:T(128)}, ...), condition=%wide.region_5.6_spmd.clone, body=%wide.region_2.5_spmd.clone.sunk | while | flops 1099955712 | bytes 35199700 | solution.py:93
  766.2 56.2 %while.32 = (s32[]{:T(128)}, f32[1,1024,4,128]{1,3,2,0:T(8,128)S(1)}, f32[1,1024,4,128]{1,3,2,0:T(8,128)}, bf16[2,1,512,4,128]{4,2,0,3,1:T(8,128)(2,1)}, s32[2]{...) while((s32[]{:T(128)}, ...), condition=%wide.region_9.10_spmd.clone, body=%wide.region_7.9_spmd.clone.sunk | while | flops 2709257728 | bytes 170966912 | solution.py:143
  830.6 24.3 %all-to-all-done.4 = bf16[1,1024,4,128]{3,2,0,1:T(4,128)(2,1)S(1)} async-done(((bf16[1,1024,4,128]{3,2,0,1:T(4,128)(2,1)}), bf16[1,1024,4,128]{3,2,0,1:T(4,128)(2,1)S(1)}, u32[]{:S(2)}, u32[]{:S(2)}) %all-to-all-start.4) | async-done | bytes 1048608 | tf_op jit(solution)/shard_map/all_to_all | solution.py:322
  859.5 14.4 convert_bitcast_fusion.1
  876.8 7.8 all-to-all-done.5
  896.6 46.3 %all-to-all-done.6 = bf16[1,1024,4,128]{3,2,0,1:T(4,128)(2,1)} async-done(((bf16[1,1024,4,128]{3,2,0,1:T(4,128)(2,1)}), bf16[1,1024,4,128]{3,2,0,1:T(4,128)(2,1)}, u32[]{:S(2)}, u32[]{:S(2)}) %all-to-all-start.6) | async-done | bytes 1048608 | tf_op jit(solution)/shard_map/all_to_all | solution.py:328
  962.4 31.7 %all-to-all-done.2 = bf16[1,1024,4,128]{3,2,0,1:T(4,128)(2,1)S(1)} async-done(((bf16[1,1024,4,128]{3,2,0,1:T(4,128)(2,1)}), bf16[1,1024,4,128]{3,2,0,1:T(4,128)(2,1)S(1)}, u32[]{:S(2)}, u32[]{:S(2)}) %all-to-all-start.2) | async-done | bytes 1048608 | tf_op jit(solution)/shard_map/all_to_all | solution.py:252
  996.8 14.7 fusion.79
  1021.3 8.1 fusion.94
  1030.1 21.9 %fusion.112 = f32[2048,6144]{1,0:T(8,128)} fusion(bf16[256,6144]{0,1:T(8,128)(2,1)} %bitcast.294, bf16[1,256,2048]{2,1,0:T(8,128)(2,1)S(1)} %copy-done.4, f32[2048]{0:T(1024)S(1)} %copy-done.33, f32[2048]{0:T(1024)S(1)} %copy-done.28, f32[256]{0:T(256)S(1)} %copy-done.37, f32[256]{0:T(256)S(1)} %copy-done.39), kind=kOutput, calls=%fused_computation.199 | convolution fusion | flops 6445596672 | bytes 54544384 | tf_op jit(solution)/shard_map/dot_general | solution.py:62
  1053.9 13.9 all-reduce.19
  1074.1 7.5 fusion.71
  1081.6 60.9 %all-reduce.28.cloned.1.call-done = (f32[6144]{0:T(1024)}, f32[2048]{0:T(1024)}, f32[2048]{0:T(1024)}, f32[2048]{0:T(1024)}, f32[2048]{0:T(1024)}, /*index=5*/f32[2048]{0:T(1024)}) async-done(((f32[6144]{0:T(1024)}, f32[2048]{0:T(1024)}, f32[2048]{0:T(1024)}, f32[2048]{0:T(1024)}, f32[2048]{0:T(1024)}, /*index=5*/f32[2048]{0:T(1024)}), (f32[6144]{0:T(1024)}, f32[2048]{0:T(1024)}, f32[2048]{0:T(1024)}, ...) | async-done | bytes 65552
  1149.6 361.0 %reduce-scatter.13.cloned.1.call-done = f32[64,2048]{1,0:T(8,128)} async-done(((f32[2048,2048]{1,0:T(8,128)}), f32[64,2048]{1,0:T(8,128)}) %reduce-scatter.13.cloned.1.call-update) | async-done | bytes 524304 | tf_op jit(solution)/shard_map/reduce_scatter | solution.py:353
  1510.6 436.6 %reduce-scatter.11.cloned.1.call-done = f32[64,6144]{1,0:T(8,128)} async-done(((f32[2048,6144]{1,0:T(8,128)}), f32[64,6144]{1,0:T(8,128)}) %reduce-scatter.11.cloned.1.call-update) | async-done | bytes 1572880 | tf_op jit(solution)/shard_map/reduce_scatter | solution.py:351
  (303 shorter events, 224.3 us)
Async XLA Ops:
  7.2 135.9 %all-gather.12.cloned.1.call-start = ((), (), s32[]{:S(2)}) async-start(), calls=%async_computation.15 | async-start | bytes 5242880 | tf_op jit(solution)/shard_map/all_gather | solution.py:268
  7.2 56.6 %copy-start.19 = (bf16[1,256,2048]{2,1,0:T(8,128)(2,1)S(1)}, bf16[1,256,2048]{2,1,0:T(8,128)(2,1)}, u32[]{:S(2)}) copy-start(bf16[1,256,2048]{2,1,0:T(8,128)(2,1)} %param.21) | copy-start | bytes 3145732
  8.8 581.7 %copy-start.38 = (f32[256]{0:T(256)}, f32[256]{0:T(256)S(1)}, u32[]{:S(2)}) copy-start(f32[256]{0:T(256)S(1)} %broadcast_multiply_fusion.1) | copy-start | bytes 3076
  10.5 580.0 %copy-start.36 = (f32[256]{0:T(256)}, f32[256]{0:T(256)S(1)}, u32[]{:S(2)}) copy-start(f32[256]{0:T(256)S(1)} %fusion.109) | copy-start | bytes 3076
  62.4 135.5 %all-gather.14.cloned.1.call-start = ((), (), s32[]{:S(2)}) async-start(), calls=%async_computation.16 | async-start | bytes 9437184 | tf_op jit(solution)/shard_map/all_gather | solution.py:264
  63.1 217.1 %all-gather.18.cloned.1.call-start = ((), (), s32[]{:S(2)}) async-start(), calls=%async_computation.19 | async-start | bytes 5242880 | tf_op jit(solution)/shard_map/all_gather | solution.py:279
  65.1 269.8 %all-gather.16.cloned.1.call-start = ((), (), s32[]{:S(2)}) async-start(), calls=%async_computation.17 | async-start | bytes 9437184 | tf_op jit(solution)/shard_map/all_gather | solution.py:266
  65.7 349.3 %all-gather.10.cloned.1.call-start = ((), (), s32[]{:S(2)}) async-start(), calls=%async_computation.14 | async-start | bytes 8650752 | tf_op jit(solution)/shard_map/all_gather | solution.py:215
  66.3 524.2 %all-gather.8.cloned.1.call-start = ((), (), s32[]{:S(2)}) async-start(), calls=%async_computation.13 | async-start | bytes 25952256 | tf_op jit(solution)/shard_map/all_gather | solution.py:213
  66.9 929.9 %reduce-scatter.9.cloned.1.call-start = ((), (), s32[]{:S(2)}) async-start(), calls=%async_computation.20 | async-start | bytes 5242880 | tf_op jit(solution)/shard_map/reduce_scatter | solution.py:285
  369.2 699.3 %reduce-scatter.15.cloned.1.call-start = ((), (), s32[]{:S(2)}) async-start(), calls=%async_computation.23 | async-start | bytes 9437184 | tf_op jit(solution)/shard_map/reduce_scatter | solution.py:292
  383.4 207.1 %copy-start.27 = (f32[2048]{0:T(1024)}, f32[2048]{0:T(1024)S(1)}, u32[]{:S(2)}) copy-start(f32[2048]{0:T(1024)S(1)} %convert_element_type.270) | copy-start | bytes 24580
  383.4 207.1 %copy-start.32 = (f32[2048]{0:T(1024)}, f32[2048]{0:T(1024)S(1)}, u32[]{:S(2)}) copy-start(f32[2048]{0:T(1024)S(1)} %convert_element_type.271) | copy-start | bytes 24580
  383.7 226.2 %copy-start.23 = (f32[256,32]{1,0:T(8,128)}, f32[256,32]{1,0:T(8,128)S(1)}, u32[]{:S(2)}) copy-start(f32[256,32]{1,0:T(8,128)S(1)} %copy.131) | copy-start | bytes 98308
  383.8 226.1 %copy-start.25 = (f32[256,32]{1,0:T(8,128)}, f32[256,32]{1,0:T(8,128)S(1)}, u32[]{:S(2)}) copy-start(f32[256,32]{1,0:T(8,128)S(1)} %copy.132) | copy-start | bytes 98308
  420.8 169.7 %copy-start.3 = (bf16[1,256,2048]{2,1,0:T(8,128)(2,1)S(1)}, bf16[1,256,2048]{2,1,0:T(8,128)(2,1)}, u32[]{:S(2)}) copy-start(bf16[1,256,2048]{2,1,0:T(8,128)(2,1)} %param.19) | copy-start | bytes 3145732
  422.3 190.6 %all-to-all-start.3 = ((bf16[1,256,16,128]{3,1,0,2:T(8,128)(2,1)}), bf16[1,256,16,128]{3,1,0,2:T(8,128)(2,1)}, u32[]{:S(2)}, u32[]{:S(2)}) async-start(bf16[1,256,16,128]{3,1,0,2:T(8,128)(2,1)} %copy.143), calls=%async_computation.4 | async-start | bytes 2097152 | tf_op jit(solution)/shard_map/all_to_all | solution.py:311
  612.8 53.9 %all-to-all-start = ((bf16[1,256,16,128]{3,1,0,2:T(8,128)(2,1)}), bf16[1,256,16,128]{3,1,0,2:T(8,128)(2,1)}, u32[]{:S(2)}, u32[]{:S(2)}) async-start(bf16[1,256,16,128]{3,1,0,2:T(8,128)(2,1)} %maximum_bitcast_fusion), calls=%async_computation | async-start | bytes 2097152 | tf_op jit(solution)/shard_map/all_to_all | solution.py:243
  622.4 66.5 %collective-permute-start = (bf16[1,256,4,128]{3,1,2,0:T(8,128)(2,1)}, bf16[1,256,4,128]{3,1,2,0:T(8,128)(2,1)S(1)}, u32[]{:S(2)}, u32[]{:S(2)}) collective-permute-start(bf16[1,256,4,128]{3,1,2,0:T(8,128)(2,1)} %get-tuple-element.302), channel_id=1, source_target_pairs={{0,1},{1,0},{2,3},{3,2},{4,5},{5,4},{6,7},{7,6},{8,9},{9,8},{10,11... | collective-permute-start | bytes 786440 | tf_op jit(solution)/shard_map/ppermute | solution.py:191
  624.3 78.9 %collective-permute-start.1 = (bf16[1,256,4,128]{3,1,2,0:T(8,128)(2,1)}, bf16[1,256,4,128]{3,1,2,0:T(8,128)(2,1)S(1)}, u32[]{:S(2)}, u32[]{:S(2)}) collective-permute-start(bf16[1,256,4,128]{3,1,2,0:T(8,128)(2,1)} %get-tuple-element.303), channel_id=1, source_target_pairs={{0,2},{1,3},{2,0},{3,1},{4,6},{5,7},{6,4},{7,5},{8,10},{9,11},{10,... | collective-permute-start | bytes 786440 | tf_op jit(solution)/shard_map/ppermute | solution.py:191
  626.7 76.5 %collective-permute-start.2 = (bf16[1,256,4,128]{3,1,2,0:T(8,128)(2,1)}, bf16[1,256,4,128]{3,1,2,0:T(8,128)(2,1)S(1)}, u32[]{:S(2)}, u32[]{:S(2)}) collective-permute-start(bf16[1,256,4,128]{3,1,2,0:T(8,128)(2,1)} %get-tuple-element.304), channel_id=1, source_target_pairs={{0,3},{1,2},{2,1},{3,0},{4,7},{5,6},{6,5},{7,4},{8,11},{9,10},{10,... | collective-permute-start | bytes 786440 | tf_op jit(solution)/shard_map/ppermute | solution.py:191
  666.7 68.1 %all-to-all-start.1 = ((bf16[1,256,16,128]{3,1,0,2:T(8,128)(2,1)}), bf16[1,256,16,128]{3,1,0,2:T(8,128)(2,1)}, u32[]{:S(2)}, u32[]{:S(2)}) async-start(bf16[1,256,16,128]{3,1,0,2:T(8,128)(2,1)} %bitcast.221), calls=%async_computation.1 | async-start | bytes 2097152 | tf_op jit(solution)/shard_map/all_to_all | solution.py:247
  672.3 399.0 %reduce-scatter.17.cloned.1.call-start = ((), (), s32[]{:S(2)}) async-start(), calls=%async_computation.24 | async-start | bytes 9437184 | tf_op jit(solution)/shard_map/reduce_scatter | solution.py:298
  825.4 29.5 %all-to-all-start.4 = ((bf16[1,1024,4,128]{3,2,0,1:T(4,128)(2,1)}), bf16[1,1024,4,128]{3,2,0,1:T(4,128)(2,1)S(1)}, u32[]{:S(2)}, u32[]{:S(2)}) async-start(bf16[1,1024,4,128]{3,2,0,1:T(4,128)(2,1)} %copy.146), calls=%async_computation.5 | async-start | bytes 2097152 | tf_op jit(solution)/shard_map/all_to_all | solution.py:322
  855.9 28.8 %all-to-all-start.5 = ((bf16[1,1024,4,128]{3,2,0,1:T(4,128)(2,1)}), bf16[1,1024,4,128]{3,2,0,1:T(4,128)(2,1)S(1)}, u32[]{:S(2)}, u32[]{:S(2)}) async-start(bf16[1,1024,4,128]{3,2,0,1:T(4,128)(2,1)} %copy.149), calls=%async_computation.6 | async-start | bytes 2097152 | tf_op jit(solution)/shard_map/all_to_all | solution.py:325
  859.4 214.6 %reduce-scatter.7.cloned.1.call-start = ((), (), s32[]{:S(2)}) async-start(), calls=%async_computation.18 | async-start | bytes 5242880 | tf_op jit(solution)/shard_map/reduce_scatter | solution.py:272
  884.7 58.3 %all-to-all-start.6 = ((bf16[1,1024,4,128]{3,2,0,1:T(4,128)(2,1)}), bf16[1,1024,4,128]{3,2,0,1:T(4,128)(2,1)}, u32[]{:S(2)}, u32[]{:S(2)}) async-start(bf16[1,1024,4,128]{3,2,0,1:T(4,128)(2,1)} %copy.151), calls=%async_computation.7 | async-start | bytes 2097152 | tf_op jit(solution)/shard_map/all_to_all | solution.py:328
  942.9 51.2 %all-to-all-start.2 = ((bf16[1,1024,4,128]{3,2,0,1:T(4,128)(2,1)}), bf16[1,1024,4,128]{3,2,0,1:T(4,128)(2,1)S(1)}, u32[]{:S(2)}, u32[]{:S(2)}) async-start(bf16[1,1024,4,128]{3,2,0,1:T(4,128)(2,1)} %copy.140), calls=%async_computation.2 | async-start | bytes 2097152 | tf_op jit(solution)/shard_map/all_to_all | solution.py:252
  946.5 196.0 %all-reduce.28.cloned.1.call-start = ((), (), s32[]{:S(2)}) async-start(), calls=%async_computation.25 | async-start | bytes 131072
  1021.2 489.4 %reduce-scatter.13.cloned.1.call-start = ((), (), s32[]{:S(2)}) async-start(), calls=%async_computation.22 | async-start | bytes 17301504 | tf_op jit(solution)/shard_map/reduce_scatter | solution.py:353
  1029.4 917.8 %reduce-scatter.11.cloned.1.call-start = ((), (), s32[]{:S(2)}) async-start(), calls=%async_computation.21 | async-start | bytes 51904512 | tf_op jit(solution)/shard_map/reduce_scatter | solution.py:351
  1143.3 804.5 %copy-start.49 = (f32[64]{0:T(128)}, f32[64]{0:T(128)S(1)}, u32[]{:S(2)}) copy-start(f32[64]{0:T(128)S(1)} %dynamic-slice.32) | copy-start | bytes 772
  (48 other events, 462.6 us)
Sparse Core Ops, SparseCore 0:
  62.5 80.5 all-gather.11
  144.9 52.9 all-gather.13
  199.5 80.7 all-gather.17
  282.0 52.9 all-gather.15
  337.7 77.2 all-gather.9
  417.8 172.6 all-gather.7
  592.8 119.8 reduce-scatter.8
  716.6 83.4 reduce-scatter.14
  803.6 71.2 reduce-scatter.16
  877.1 109.9 reduce-scatter.6
  1021.4 121.0 all-reduce.27
  1145.2 365.3 reduce-scatter.12
  1517.6 429.5 reduce-scatter.10
